TPU v7x, 512 devices: a whole 4x4x16 slice. The times are simulated.
512 devices in a mesh: tm: 128 (over y, x_hi, z), col: 4 (over x_lo, core).
Axes of the slice: x: 4 (x_hi: 2, x_lo: 2; x = x_hi * 2 + x_lo), y: 4, z: 16, core: 2. Of those that a mesh axis runs over, the one named last changes fastest.
Arguments:
- frames: bfloat16 [384, 2, 96, 384], P('tm', None, 'col'), may hold values from -6 to 6
- up_kernel: bfloat16 [10368, 256], P(None, 'tm'), may hold values from -0.109375 to 0.109375
- mix_kernel: bfloat16 [6912, 256], P(None, 'tm'), may hold values from -0.078125 to 0.078125
- cotangent: bfloat16 [768, 2, 96, 256], P('tm', None, 'col'), may hold values from -6 to 6
Outputs:
- decoded: bfloat16 [768, 2, 96, 256], P('tm', None, 'col')
- frames_grad: bfloat16 [384, 2, 96, 384], P('tm', None, 'col')
All inputs are finite; a program needn't handle non-finite values.
Results may differ from a plain program's by a relative error of at most 0.005.
Values may be sent and summed in bfloat16 or wider, within the bound.
No kernel may reach another device: no remote copies, remote signals or barrier semaphores. Data moves between devices by JAX's collectives and lax.ppermute only.
A program may use at most 64 MiB of HBM per device.

v0:
```python
import jax
import jax.numpy as jnp
from jax import lax
from jax.sharding import PartitionSpec as P


def with_halo(block, sides, width):
    for axis, dim in sides:
        count = lax.axis_size(axis)
        forward = [(i, i + 1) for i in range(count - 1)]
        backward = [(target, source) for source, target in forward]
        low = lax.ppermute(
            lax.slice_in_dim(block, block.shape[dim] - width, None, axis=dim), axis, forward
        )
        high = lax.ppermute(lax.slice_in_dim(block, 0, width, axis=dim), axis, backward)
        block = jnp.concatenate([low, block, high], axis=dim)
    return block


def from_behind(array, axis, by):
    devices = lax.axis_size(axis)
    pairs = [(i, i + by) for i in range(devices) if 0 <= i + by < devices]
    return lax.ppermute(array, axis, pairs)


def widen(field):
    return with_halo(field, (("col", 2),), 1)


def from_previous(field):
    return from_behind(field, "tm", 1)


def from_next(field):
    return from_behind(field, "tm", -1)


def forward_pass(kernel, produce):
    return produce(lax.all_gather(kernel, "tm", axis=1, tiled=True), jnp.int32(0))


def backward_pass(kernel, combine, initial):
    return combine(initial, lax.all_gather(kernel, "tm", axis=1, tiled=True), jnp.int32(0))


def pad_rows(field):
    return jnp.pad(field, ((0, 0), (1, 1), (0, 0), (0, 0)))


def window(padded, first, count, row_low, col_low, height, width):
    part = padded[first : first + count, row_low : row_low + height, col_low : col_low + width]
    return part.reshape(-1, part.shape[-1])


def transposed(rows, matrix):
    return lax.dot_general(
        rows, matrix, (((1,), (1,)), ((), ())), preferred_element_type=jnp.float32
    )


def shards(frames, up_kernel, mix_kernel, cotangent):
    frame_count, height, width, in_channels = frames.shape
    out_channels = mix_kernel.shape[0] // 27
    count = 2 * frame_count
    block = count * height * width
    widened = widen(frames)
    earlier = from_previous(widened[-1:])
    extended = pad_rows(jnp.concatenate((earlier, widened), axis=0))
    rows_in = extended.shape[0] - 1

    def up_columns(piece, start):
        taps = piece.reshape(3, 3, 3, in_channels, piece.shape[1])
        even = jnp.zeros((rows_in * height * width, piece.shape[1]), jnp.float32)
        odd = even
        for tap_h in range(3):
            for tap_w in range(3):
                current = window(extended, 1, rows_in, tap_h, tap_w, height, width)
                prior = window(extended, 0, rows_in, tap_h, tap_w, height, width)
                even = even + jnp.dot(
                    current, taps[0, tap_h, tap_w], preferred_element_type=jnp.float32
                )
                even = even + jnp.dot(
                    prior, taps[2, tap_h, tap_w], preferred_element_type=jnp.float32
                )
                odd = odd + jnp.dot(
                    current, taps[1, tap_h, tap_w], preferred_element_type=jnp.float32
                )
        stacked = jnp.stack(
            (even.reshape(rows_in, height * width, -1), odd.reshape(rows_in, height * width, -1)),
            axis=1,
        )
        return stacked.reshape(-1, piece.shape[1])

    before_all = forward_pass(up_kernel, up_columns).reshape(
        2 * rows_in, height, width, out_channels
    )
    hidden = jax.nn.silu(before_all).astype(jnp.bfloat16)
    earlier_hidden = from_previous(hidden[-2:])
    hidden_pad = pad_rows(widen(jnp.concatenate((earlier_hidden, hidden), axis=0)))
    cot_pad = pad_rows(widen(jnp.concatenate((cotangent, from_next(cotangent[:2])), axis=0)))

    def mix_forward(piece, start):
        taps = piece.reshape(3, 3, 3, out_channels, piece.shape[1])
        total = jnp.zeros((block, piece.shape[1]), jnp.float32)
        for tap_t in range(3):
            for tap_h in range(3):
                for tap_w in range(3):
                    total = total + jnp.dot(
                        window(hidden_pad, tap_t, count, tap_h, tap_w, height, width),
                        taps[tap_t, tap_h, tap_w],
                        preferred_element_type=jnp.float32,
                    )
        return total

    def mix_backward(piece):
        taps = piece.reshape(3, 3, 3, out_channels, piece.shape[1])
        total = jnp.zeros((block, out_channels), jnp.float32)
        for tap_t in range(3):
            for tap_h in range(3):
                for tap_w in range(3):
                    total = total + transposed(
                        window(cot_pad, 2 - tap_t, count, 2 - tap_h, 2 - tap_w, height, width),
                        taps[tap_t, tap_h, tap_w],
                    )
        return total

    empty = jnp.zeros((block, out_channels), jnp.float32)
    decoded_flat = forward_pass(mix_kernel, mix_forward)

    def accumulate(total, piece, start):
        return mix_backward(piece)

    hidden_grad = backward_pass(mix_kernel, accumulate, empty)
    flat_before = before_all.reshape(block, out_channels)
    sigma = jax.nn.sigmoid(flat_before)
    before_grad = (hidden_grad * sigma * (1.0 + flat_before * (1.0 - sigma))).astype(jnp.bfloat16)
    before_grad = before_grad.reshape(count, height, width, out_channels)
    grad_pad = pad_rows(widen(jnp.concatenate((before_grad, from_next(before_grad[:1])), axis=0)))
    evens = grad_pad[0::2]
    odds = grad_pad[1::2]

    def up_backward(total, piece, start):
        taps = piece.reshape(3, 3, 3, in_channels, piece.shape[1])
        for tap_h in range(3):
            for tap_w in range(3):
                total = total + transposed(
                    window(evens, 0, frame_count, 2 - tap_h, 2 - tap_w, height, width),
                    taps[0, tap_h, tap_w],
                )
                total = total + transposed(
                    window(odds, 0, frame_count, 2 - tap_h, 2 - tap_w, height, width),
                    taps[1, tap_h, tap_w],
                )
                total = total + transposed(
                    window(evens, 1, frame_count, 2 - tap_h, 2 - tap_w, height, width),
                    taps[2, tap_h, tap_w],
                )
        return total

    grad_start = jnp.zeros((frame_count * height * width, in_channels), jnp.float32)
    grad_total = backward_pass(up_kernel, up_backward, grad_start)
    decoded = decoded_flat.astype(jnp.bfloat16).reshape(count, height, width, out_channels)
    frames_grad = grad_total.astype(jnp.bfloat16).reshape(frame_count, height, width, in_channels)
    return (decoded, frames_grad)


def solution(mesh):
    placed = (P("tm", None, "col", None), P(None, "tm"), P(None, "tm"), P("tm", None, "col", None))
    return jax.shard_map(
        shards,
        mesh=mesh,
        in_specs=placed,
        out_specs=(P("tm", None, "col", None), P("tm", None, "col", None)),
        check_vma=False,
    )
```

profile of v0, /device:TPU:1, one launch (start us, length us, event | category | flops | bytes accessed | tf_op | source)
XLA Modules:
  0.0 542.3 jit_solution(755618982540305264)
XLA Ops:
  9.5 8.8 %collective-permute-start.1 = (bf16[3,2,1,384]{3,2,1,0:T(2,128)(2,1)S(1)}, bf16[3,2,1,384]{3,2,1,0:T(2,128)(2,1)S(1)}, u32[]{:S(2)}, u32[]{:S(2)}) collective-permute-start(bf16[3,2,1,384]{3,2,1,0:T(2,128)(2,1)S(1)} %get-tuple-element.114), channel_id=1, source_target_pairs={{1,0},{2,1},{3,2},{5,4},{6,5},{7,6},{9,8},{10,9},{11,10},{13,12},{... | collective-permute-start | bytes 13832 | tf_op jit(solution)/shard_map/ppermute | solution.py:15
  18.3 1.9 collective-permute-start
  21.0 1.3 collective-permute-start.6
  24.0 4.0 collective-permute-start.2
  28.0 1.7 pad_maximum_fusion.5
  30.8 3.0 collective-permute-start.8
  33.8 2.6 collective-permute-start.7
  36.4 1.2 pad_slice_fusion
  38.9 1.5 fusion.45
  40.5 188.4 %all-gather.7.cloned.1.call-done = bf16[128,2,6912]{2,1,0:T(2,128)(2,1)} async-done(((bf16[1,2,6912]{2,1,0:T(2,128)(2,1)}), bf16[128,2,6912]{2,1,0:T(2,128)(2,1)}) %all-gather.7.cloned.1.call-update) | async-done | bytes 3538960 | tf_op jit(solution)/shard_map/all_gather | solution.py:39
  228.9 8.3 %reshape.429 = bf16[256,6912]{1,0:T(8,128)(2,1)} reshape(bf16[128,2,6912]{2,1,0:T(2,128)(2,1)} %all-gather.7.cloned.1.call-done) | data formatting | bytes 7077888
  237.1 5.0 copy.18
  242.2 1.2 fusion.44
  256.8 200.9 %all-gather.5.cloned.1.call-done = bf16[128,2,10368]{2,1,0:T(2,128)(2,1)} async-done(((bf16[1,2,10368]{2,1,0:T(2,128)(2,1)}), bf16[128,2,10368]{2,1,0:T(2,128)(2,1)}) %all-gather.5.cloned.1.call-update) | async-done | bytes 5308432 | tf_op jit(solution)/shard_map/all_gather | solution.py:39
  457.7 7.9 %reshape.427 = bf16[256,10368]{1,0:T(8,128)(2,1)} reshape(bf16[128,2,10368]{2,1,0:T(2,128)(2,1)} %all-gather.5.cloned.1.call-done) | data formatting | bytes 10616832
  465.6 8.0 %copy.15 = bf16[10368,256]{1,0:T(8,128)(2,1)} copy(bf16[10368,256]{0,1:T(8,128)(2,1)} %bitcast.565) | data formatting | bytes 10616832
  473.7 1.3 fusion.30
  475.0 1.7 fusion.27
  477.9 1.2 fusion.31
  479.1 1.2 fusion.29
  481.5 1.2 convolution_add_fusion.78
  482.7 1.2 convolution_add_fusion.93
  483.9 1.2 convolution_add_fusion.92
  485.1 1.2 convolution_add_fusion.77
  491.3 1.3 collective-permute-start.9
  492.6 3.3 collective-permute-done.9
  495.9 12.7 %collective-permute-start.11 = (bf16[7,2,1,256]{3,2,1,0:T(2,128)(2,1)S(1)}, bf16[7,2,1,256]{3,2,1,0:T(2,128)(2,1)S(1)}, u32[]{:S(2)}, u32[]{:S(2)}) collective-permute-start(bf16[7,2,1,256]{3,2,1,0:T(2,128)(2,1)S(1)} %get-tuple-element.110), channel_id=1, source_target_pairs={{1,0},{2,1},{3,2},{5,4},{6,5},{7,6},{9,8},{10,9},{11,10},{13,12},{... | collective-permute-start | bytes 21512 | tf_op jit(solution)/shard_map/ppermute | solution.py:15
  508.7 2.1 collective-permute-start.10
  510.9 2.9 collective-permute-start.3
  521.0 2.7 collective-permute-start.4
  523.7 1.9 collective-permute-start.5
  525.7 3.1 collective-permute-done.5
  (205 shorter events, 40.8 us)
Async XLA Ops:
  7.2 221.7 %all-gather.7.cloned.1.call-start = ((), (), s32[]{:S(2)}) async-start(), calls=%async_computation.1 | async-start | bytes 3566592 | tf_op jit(solution)/shard_map/all_gather | solution.py:39
  7.9 449.8 %all-gather.5.cloned.1.call-start = ((), (), s32[]{:S(2)}) async-start(), calls=%async_computation | async-start | bytes 5349888 | tf_op jit(solution)/shard_map/all_gather | solution.py:39
  9.5 13.7 %collective-permute-start.1 = (bf16[3,2,1,384]{3,2,1,0:T(2,128)(2,1)S(1)}, bf16[3,2,1,384]{3,2,1,0:T(2,128)(2,1)S(1)}, u32[]{:S(2)}, u32[]{:S(2)}) collective-permute-start(bf16[3,2,1,384]{3,2,1,0:T(2,128)(2,1)S(1)} %get-tuple-element.114), channel_id=1, source_target_pairs={{1,0},{2,1},{3,2},{5,4},{6,5},{7,6},{9,8},{10,9},{11,10},{13,12},{... | collective-permute-start | bytes 13832 | tf_op jit(solution)/shard_map/ppermute | solution.py:15
  18.3 5.0 collective-permute-start
  21.0 9.8 %collective-permute-start.6 = (bf16[2,2,24,256]{3,2,1,0:T(8,128)(2,1)S(1)}, bf16[2,2,24,256]{3,2,1,0:T(8,128)(2,1)S(1)}, u32[]{:S(2)}, u32[]{:S(2)}) collective-permute-start(bf16[2,2,24,256]{3,2,1,0:T(8,128)(2,1)S(1)} %slice.702), channel_id=1, source_target_pairs={{4,0},{8,4},{12,8},{16,12},{20,16},{24,20},{28,24},{32,28},{36,32}... | collective-permute-start | bytes 147464 | tf_op jit(solution)/shard_map/ppermute | solution.py:23
  24.0 5.7 %collective-permute-start.2 = (bf16[1,2,26,384]{3,2,1,0:T(8,128)(2,1)S(1)}, bf16[1,2,26,384]{3,2,1,0:T(8,128)(2,1)S(1)}, u32[]{:S(2)}, u32[]{:S(2)}) collective-permute-start(bf16[1,2,26,384]{3,2,1,0:T(8,128)(2,1)S(1)} %pad_maximum_fusion.7), channel_id=1, source_target_pairs={{0,4},{4,8},{8,12},{12,16},{16,20},{20,24},{24,28},{28,32},{32,36}... | collective-permute-start | bytes 119816 | tf_op jit(solution)/shard_map/ppermute | solution.py:23
  30.8 6.8 %collective-permute-start.8 = (bf16[8,2,1,256]{3,2,1,0:T(2,128)(2,1)S(1)}, bf16[8,2,1,256]{3,2,1,0:T(2,128)(2,1)S(1)}, u32[]{:S(2)}, u32[]{:S(2)}) collective-permute-start(bf16[8,2,1,256]{3,2,1,0:T(2,128)(2,1)S(1)} %get-tuple-element.87), channel_id=1, source_target_pairs={{1,0},{2,1},{3,2},{5,4},{6,5},{7,6},{9,8},{10,9},{11,10},{13,12},{... | collective-permute-start | bytes 24584 | tf_op jit(solution)/shard_map/ppermute | solution.py:15
  33.8 3.9 collective-permute-start.7
  242.1 9.5 %copy-start.12 = (bf16[6,2,24,256]{3,2,1,0:T(8,128)(2,1)S(1)}, bf16[6,2,24,256]{3,2,1,0:T(8,128)(2,1)}, u32[]{:S(2)}) copy-start(bf16[6,2,24,256]{3,2,1,0:T(8,128)(2,1)} %get-tuple-element.85) | copy-start | bytes 442372
  242.1 9.7 %copy-start.27 = (bf16[6,2,24,256]{3,2,1,0:T(8,128)(2,1)S(1)}, bf16[6,2,24,256]{3,2,1,0:T(8,128)(2,1)}, u32[]{:S(2)}) copy-start(bf16[6,2,24,256]{3,2,1,0:T(8,128)(2,1)} %get-tuple-element.16) | copy-start | bytes 442372
  242.1 10.0 %copy-start.26 = (bf16[6,2,24,256]{3,2,1,0:T(8,128)(2,1)S(1)}, bf16[6,2,24,256]{3,2,1,0:T(8,128)(2,1)}, u32[]{:S(2)}) copy-start(bf16[6,2,24,256]{3,2,1,0:T(8,128)(2,1)} %get-tuple-element.15) | copy-start | bytes 442372
  242.1 10.2 %copy-start.25 = (bf16[6,2,24,256]{3,2,1,0:T(8,128)(2,1)S(1)}, bf16[6,2,24,256]{3,2,1,0:T(8,128)(2,1)}, u32[]{:S(2)}) copy-start(bf16[6,2,24,256]{3,2,1,0:T(8,128)(2,1)} %get-tuple-element.14) | copy-start | bytes 442372
  242.1 10.5 %copy-start.24 = (bf16[6,2,24,256]{3,2,1,0:T(8,128)(2,1)S(1)}, bf16[6,2,24,256]{3,2,1,0:T(8,128)(2,1)}, u32[]{:S(2)}) copy-start(bf16[6,2,24,256]{3,2,1,0:T(8,128)(2,1)} %get-tuple-element.13) | copy-start | bytes 442372
  242.2 10.7 %copy-start.23 = (bf16[6,2,24,256]{3,2,1,0:T(8,128)(2,1)S(1)}, bf16[6,2,24,256]{3,2,1,0:T(8,128)(2,1)}, u32[]{:S(2)}) copy-start(bf16[6,2,24,256]{3,2,1,0:T(8,128)(2,1)} %get-tuple-element.12) | copy-start | bytes 442372
  243.4 9.7 %copy-start.22 = (bf16[6,2,24,256]{3,2,1,0:T(8,128)(2,1)S(1)}, bf16[6,2,24,256]{3,2,1,0:T(8,128)(2,1)}, u32[]{:S(2)}) copy-start(bf16[6,2,24,256]{3,2,1,0:T(8,128)(2,1)} %get-tuple-element.11) | copy-start | bytes 442372
  244.6 8.8 %copy-start.13 = (bf16[6,2,24,256]{3,2,1,0:T(8,128)(2,1)S(1)}, bf16[6,2,24,256]{3,2,1,0:T(8,128)(2,1)}, u32[]{:S(2)}) copy-start(bf16[6,2,24,256]{3,2,1,0:T(8,128)(2,1)} %get-tuple-element.81) | copy-start | bytes 442372
  473.6 13.9 %copy-start = (bf16[10368,256]{1,0:T(8,128)(2,1)S(1)}, bf16[10368,256]{1,0:T(8,128)(2,1)}, u32[]{:S(2)}) copy-start(bf16[10368,256]{1,0:T(8,128)(2,1)} %copy.15) | copy-start | bytes 15925252
  473.6 13.9 %copy-start.6 = (bf16[3,2,24,384]{3,2,1,0:T(8,128)(2,1)S(1)}, bf16[3,2,24,384]{3,2,1,0:T(8,128)(2,1)}, u32[]{:S(2)}) copy-start(bf16[3,2,24,384]{3,2,1,0:T(8,128)(2,1)} %get-tuple-element.98) | copy-start | bytes 331780
  473.6 14.1 %copy-start.32 = (bf16[3,2,24,384]{3,2,1,0:T(8,128)(2,1)S(1)}, bf16[3,2,24,384]{3,2,1,0:T(8,128)(2,1)}, u32[]{:S(2)}) copy-start(bf16[3,2,24,384]{3,2,1,0:T(8,128)(2,1)} %get-tuple-element.99) | copy-start | bytes 331780
  473.6 14.3 %copy-start.8 = (bf16[3,2,24,384]{3,2,1,0:T(8,128)(2,1)S(1)}, bf16[3,2,24,384]{3,2,1,0:T(8,128)(2,1)}, u32[]{:S(2)}) copy-start(bf16[3,2,24,384]{3,2,1,0:T(8,128)(2,1)} %get-tuple-element.112) | copy-start | bytes 331780
  473.6 14.6 %copy-start.1 = (bf16[3,2,24,384]{3,2,1,0:T(8,128)(2,1)S(1)}, bf16[3,2,24,384]{3,2,1,0:T(8,128)(2,1)}, u32[]{:S(2)}) copy-start(bf16[3,2,24,384]{3,2,1,0:T(8,128)(2,1)} %param.4) | copy-start | bytes 331780
  473.6 14.8 %copy-start.31 = (bf16[3,2,24,384]{3,2,1,0:T(8,128)(2,1)S(1)}, bf16[3,2,24,384]{3,2,1,0:T(8,128)(2,1)}, u32[]{:S(2)}) copy-start(bf16[3,2,24,384]{3,2,1,0:T(8,128)(2,1)} %get-tuple-element.106) | copy-start | bytes 331780
  473.6 15.0 %copy-start.7 = (bf16[3,2,24,384]{3,2,1,0:T(8,128)(2,1)S(1)}, bf16[3,2,24,384]{3,2,1,0:T(8,128)(2,1)}, u32[]{:S(2)}) copy-start(bf16[3,2,24,384]{3,2,1,0:T(8,128)(2,1)} %get-tuple-element.111) | copy-start | bytes 331780
  473.6 15.2 %copy-start.3 = (bf16[3,2,24,384]{3,2,1,0:T(8,128)(2,1)S(1)}, bf16[3,2,24,384]{3,2,1,0:T(8,128)(2,1)}, u32[]{:S(2)}) copy-start(bf16[3,2,24,384]{3,2,1,0:T(8,128)(2,1)} %get-tuple-element.100) | copy-start | bytes 331780
  477.9 11.5 %copy-start.5 = (bf16[3,2,24,384]{3,2,1,0:T(8,128)(2,1)S(1)}, bf16[3,2,24,384]{3,2,1,0:T(8,128)(2,1)}, u32[]{:S(2)}) copy-start(bf16[3,2,24,384]{3,2,1,0:T(8,128)(2,1)} %get-tuple-element.102) | copy-start | bytes 331780
  479.1 10.5 %copy-start.30 = (bf16[3,2,24,384]{3,2,1,0:T(8,128)(2,1)S(1)}, bf16[3,2,24,384]{3,2,1,0:T(8,128)(2,1)}, u32[]{:S(2)}) copy-start(bf16[3,2,24,384]{3,2,1,0:T(8,128)(2,1)} %get-tuple-element.101) | copy-start | bytes 331780
  491.3 4.6 collective-permute-start.9
  495.9 17.9 %collective-permute-start.11 = (bf16[7,2,1,256]{3,2,1,0:T(2,128)(2,1)S(1)}, bf16[7,2,1,256]{3,2,1,0:T(2,128)(2,1)S(1)}, u32[]{:S(2)}, u32[]{:S(2)}) collective-permute-start(bf16[7,2,1,256]{3,2,1,0:T(2,128)(2,1)S(1)} %get-tuple-element.110), channel_id=1, source_target_pairs={{1,0},{2,1},{3,2},{5,4},{6,5},{7,6},{9,8},{10,9},{11,10},{13,12},{... | collective-permute-start | bytes 21512 | tf_op jit(solution)/shard_map/ppermute | solution.py:15
  508.7 5.1 collective-permute-start.10
  510.9 10.1 %collective-permute-start.3 = (bf16[2,2,24,256]{3,2,1,0:T(8,128)(2,1)S(1)}, bf16[2,2,24,256]{3,2,1,0:T(8,128)(2,1)S(1)}, u32[]{:S(2)}, u32[]{:S(2)}) collective-permute-start(bf16[2,2,24,256]{3,2,1,0:T(8,128)(2,1)S(1)} %slice.794), channel_id=1, source_target_pairs={{0,4},{4,8},{8,12},{12,16},{16,20},{20,24},{24,28},{28,32},{32,36}... | collective-permute-start | bytes 147464 | tf_op jit(solution)/shard_map/ppermute | solution.py:23
  521.0 4.7 collective-permute-start.4
  523.7 5.1 collective-permute-start.5
  (15 other events, 62.8 us)
Sparse Core Ops, SparseCore 0:
  12.5 216.3 all-gather.6
  233.4 224.2 all-gather.4
where the time goes:
time: 544 us; the launch traced here: 542 us
  waiting for transfers between devices  397 us (73%)
  starting transfers between devices  45.2 us (8%)
  matrix products  43.6 us (8%)
  local copies, waits for them, and re-layouts  35.3 us (6%)
  between operations  15.6 us (3%)
  other arithmetic  5.54 us (1%)
    all_gather x2, waiting for transfers between devices, forward_pass(): lax.all_gather(kernel, 'tm', axis=1, tiled=True)  389 us
    unnamed x71, local copies, waits for them, and re-layouts  30.2 us
    ppermute x4, starting transfers between devices, with_halo(): lax.ppermute(lax.slice_in_dim(block, 0, width, axis=dim), axis, backward)  26.4 us
    dot_general x54, matrix products, transposed(): lax.dot_general(rows, matrix, (((1,), (1,)), ((), ())), preferred_element...  21 us
  transfers between devices with their start and end apart: 14, of which 4 were waited for; matrix products, arithmetic and copies ran while one was open for 8% of the time, Pallas kernels for 0%

commit v1 on v0

--- a/solution.py
+++ b/solution.py
@@ -36,7 +36,12 @@
 
 
 def forward_pass(kernel, produce):
-    return produce(lax.all_gather(kernel, "tm", axis=1, tiled=True), jnp.int32(0))
+    return produce(
+        jnp.concatenate(
+            lax.all_to_all(jnp.stack([kernel] * lax.axis_size("tm")), "tm", 0, 0), axis=1
+        ),
+        jnp.int32(0),
+    )
 
 
 def backward_pass(kernel, combine, initial):

time: 544 us -> 953 us (1.75)
  blocking collectives: 0 us -> 179 us
  local copies, waits for them, and re-layouts: 35.3 us -> 185 us
  waiting for transfers between devices: 397 us -> 449 us
  starting transfers between devices: 45.2 us -> 59.9 us
    ppermute x4, waiting for transfers between devices: 3.28 us -> 220 us  [from_behind(): return lax.ppermute(array, axis, pairs)]
    all_to_all x0 -> x1, blocking collectives: none -> 179 us  [forward_pass(): lax.all_to_all(jnp.stack([kernel] * lax.axis_size('tm')), 'tm', 0, 0)]
    all_gather x2, waiting for transfers between devices: 389 us -> 225 us  [backward_pass(): lax.all_gather(kernel, 'tm', axis=1, tiled=True)]
    slice x0 -> x58, local copies, waits for them, and re-layouts: none -> 114 us  [the longest x29 45.5 us: mix_forward(): taps[tap_t, tap_h, tap_w]]
    another operation x0 -> x4, local copies, waits for them, and re-layouts: none -> 37.3 us  [the longest x1 17.3 us: up_columns(): taps = piece.reshape(3, 3, 3, in_channels, piece.shape[1])]
    all_to_all x0 -> x1, starting transfers between devices: none -> 14.4 us  [forward_pass(): lax.all_to_all(jnp.stack([kernel] * lax.axis_size('tm')), 'tm', 0, 0)]
    unnamed x71 -> x171, local copies, waits for them, and re-layouts: 30.2 us -> 30.3 us
  transfers between devices with their start and end apart: 14 -> 15, of which waited for: 4 -> 5; matrix products, arithmetic and copies ran while one was open for 8% -> 12% of each run, Pallas kernels for 0% -> 0%
where the time goes in v1:
time: 953 us; the launch traced here: 943 us
  waiting for transfers between devices  449 us (47%)
  local copies, waits for them, and re-layouts  185 us (19%)
  blocking collectives  179 us (19%)
  starting transfers between devices  59.9 us (6%)
  matrix products  48.4 us (5%)
  between operations  16.6 us (2%)
    all_gather x2, waiting for transfers between devices, backward_pass(): lax.all_gather(kernel, 'tm', axis=1, tiled=True)  225 us
    ppermute x4, waiting for transfers between devices, from_behind(): return lax.ppermute(array, axis, pairs)  220 us
    all_to_all x1, blocking collectives, forward_pass(): lax.all_to_all(jnp.stack([kernel] * lax.axis_size('tm')), 'tm', 0, 0)  179 us
    slice x29, local copies, waits for them, and re-layouts, mix_forward(): taps[tap_t, tap_h, tap_w]  45.5 us
    unnamed x171, local copies, waits for them, and re-layouts  30.3 us
    slice x10, local copies, waits for them, and re-layouts, up_columns(): taps[2, tap_h, tap_w]  29.3 us
    ppermute x4, starting transfers between devices, with_halo(): lax.ppermute(lax.slice_in_dim(block, 0, width, axis=dim), axis, backward)  24.7 us
    dot_general x54, matrix products, transposed(): lax.dot_general(rows, matrix, (((1,), (1,)), ((), ())), preferred_element...  23.7 us
  transfers between devices with their start and end apart: 15, of which 5 were waited for; matrix products, arithmetic and copies ran while one was open for 12% of the time, Pallas kernels for 0%

profile of v1, /device:TPU:1, one launch (start us, length us, event | category | flops | bytes accessed | tf_op | source)
XLA Modules:
  0.0 942.5 jit_solution(14279617166301909395)
XLA Ops:
  7.2 2.6 stack.8
  9.8 179.3 %all_to_all.10 = bf16[128,6912,2]{1,2,0:T(2,128)(2,1)} all-to-all(bf16[128,6912,2]{1,2,0:T(2,128)(2,1)S(1)} %stack.8), channel_id=1, replica_groups=mesh['tm'=128,'col'=4] {'tm'}, dimensions={0} | all-to-all | bytes 7077888 | tf_op jit(solution)/shard_map/all_to_all | solution.py:41
  189.1 5.1 stack.6
  194.2 14.4 %all-to-all-start = ((bf16[128,10368,2]{1,2,0:T(2,128)(2,1)}), bf16[128,10368,2]{1,2,0:T(2,128)(2,1)}, u32[]{:S(2)}, u32[]{:S(2)}) async-start(bf16[128,10368,2]{1,2,0:T(2,128)(2,1)} %stack.6), calls=%async_computation | async-start | bytes 10616832 | tf_op jit(solution)/shard_map/all_to_all | solution.py:41
  210.1 3.3 collective-permute-start.1
  213.5 2.2 collective-permute-start
  217.1 4.0 collective-permute-start.2
  221.9 213.3 %collective-permute-done.2 = bf16[1,2,26,384]{3,2,1,0:T(8,128)(2,1)S(1)} collective-permute-done((bf16[1,2,26,384]{3,2,1,0:T(8,128)(2,1)S(1)}, bf16[1,2,26,384]{3,2,1,0:T(8,128)(2,1)S(1)}, u32[]{:S(2)}, u32[]{:S(2)}) %collective-permute-start.2) | collective-permute-done | bytes 39968 | tf_op jit(solution)/shard_map/ppermute | solution.py:23
  435.2 6.5 collective-permute-done.6
  441.7 7.9 collective-permute-start.8
  449.6 2.1 collective-permute-start.7
  455.9 26.3 %all-gather.5.cloned.1.call-done = bf16[128,2,6912]{2,1,0:T(2,128)(2,1)} async-done(((bf16[1,2,6912]{2,1,0:T(2,128)(2,1)}), bf16[128,2,6912]{2,1,0:T(2,128)(2,1)}) %all-gather.5.cloned.1.call-update) | async-done | bytes 3538960 | tf_op jit(solution)/shard_map/all_gather | solution.py:48
  482.2 8.7 reshape.437
  490.9 5.0 copy.127
  510.6 198.7 %all-gather.7.cloned.1.call-done = bf16[128,2,10368]{2,1,0:T(2,128)(2,1)} async-done(((bf16[1,2,10368]{2,1,0:T(2,128)(2,1)}), bf16[128,2,10368]{2,1,0:T(2,128)(2,1)}) %all-gather.7.cloned.1.call-update) | async-done | bytes 5308432 | tf_op jit(solution)/shard_map/all_gather | solution.py:48
  709.3 7.9 reshape.439
  717.2 8.0 copy.128
  725.2 12.3 %reshape_reshape.11 = bf16[3,3,3,256,256]{3,2,1,0,4:T(4,128)(2,1)} reshape(bf16[6912,128,2]{0,2,1:T(2,128)(2,1)} %bitcast.629) | data formatting | bytes 7077888 | tf_op jit(solution)/shard_map/reshape;reshape | solution.py:108
  737.5 8.9 fusion.101
  746.4 17.3 %reshape_reshape.9 = bf16[3,3,3,384,256]{3,2,1,0,4:T(4,128)(2,1)} reshape(bf16[10368,128,2]{0,2,1:T(2,128)(2,1)} %bitcast.1) | data formatting | bytes 10616832 | tf_op jit(solution)/shard_map/reshape;reshape | solution.py:77
  763.8 12.9 %fusion.99 = (bf16[1,1,1,384,256]{3,2,1,0,4:T(2,128)(2,1)}, bf16[1,1,1,384,256]{3,2,1,0,4:T(2,128)(2,1)}, bf16[1,1,1,384,256]{3,2,1,0,4:T(2,128)(2,1)}, bf16[1,1...) fusion(bf16[3,3,3,384,256]{3,2,1,0,4:T(4,128)(2,1)} %reshape_re, ...), kind=kLoop, calls=%fused_computation.300 | loop fusion | bytes 7471104 | tf_op jit(solution)/shard_map/slice | solution.py:88
  776.7 6.0 fusion.100
  782.6 1.8 copy.95
  795.4 1.8 copy.96
  808.2 1.8 copy.72
  855.0 4.5 fusion.102
  891.9 11.6 %collective-permute-start.11 = (bf16[7,2,1,256]{3,2,1,0:T(2,128)(2,1)S(1)}, bf16[7,2,1,256]{3,2,1,0:T(2,128)(2,1)S(1)}, u32[]{:S(2)}, u32[]{:S(2)}) collective-permute-start(bf16[7,2,1,256]{3,2,1,0:T(2,128)(2,1)S(1)} %get-tuple-element.164), channel_id=1, source_target_pairs={{1,0},{2,1},{3,2},{5,4},{6,5},{7,6},{9,8},{10,9},{11,10},{13,12},{... | collective-permute-start | bytes 21512 | tf_op jit(solution)/shard_map/ppermute | solution.py:15
  903.4 2.1 collective-permute-start.10
  905.7 4.7 collective-permute-start.3
  920.5 2.8 collective-permute-start.4
  923.3 1.9 collective-permute-start.5
  925.3 3.1 collective-permute-done.5
  (371 shorter events, 137.0 us)
Async XLA Ops:
  7.2 181.9 %copy-start.80 = (bf16[10368,2]{0,1:T(2,128)(2,1)S(1)}, bf16[10368,2]{0,1:T(2,128)(2,1)}, u32[]{:S(2)}) copy-start(bf16[10368,2]{0,1:T(2,128)(2,1)} %param.5) | copy-start | bytes 124420
  194.2 15.9 %copy-start = (bf16[3,2,24,384]{3,2,1,0:T(8,128)(2,1)S(1)}, bf16[3,2,24,384]{3,2,1,0:T(8,128)(2,1)}, u32[]{:S(2)}) copy-start(bf16[3,2,24,384]{3,2,1,0:T(8,128)(2,1)} %param.4) | copy-start | bytes 331780
  194.2 21.6 %copy-start.19 = (bf16[6,2,24,256]{3,2,1,0:T(8,128)(2,1)S(1)}, bf16[6,2,24,256]{3,2,1,0:T(8,128)(2,1)}, u32[]{:S(2)}) copy-start(bf16[6,2,24,256]{3,2,1,0:T(8,128)(2,1)} %param.7) | copy-start | bytes 442372
  194.2 552.3 %all-to-all-start = ((bf16[128,10368,2]{1,2,0:T(2,128)(2,1)}), bf16[128,10368,2]{1,2,0:T(2,128)(2,1)}, u32[]{:S(2)}, u32[]{:S(2)}) async-start(bf16[128,10368,2]{1,2,0:T(2,128)(2,1)} %stack.6), calls=%async_computation | async-start | bytes 10616832 | tf_op jit(solution)/shard_map/all_to_all | solution.py:41
  208.6 273.6 %all-gather.5.cloned.1.call-start = ((), (), s32[]{:S(2)}) async-start(), calls=%async_computation.2 | async-start | bytes 3566592 | tf_op jit(solution)/shard_map/all_gather | solution.py:48
  209.3 499.9 %all-gather.7.cloned.1.call-start = ((), (), s32[]{:S(2)}) async-start(), calls=%async_computation.3 | async-start | bytes 5349888 | tf_op jit(solution)/shard_map/all_gather | solution.py:48
  210.1 6.9 collective-permute-start.1
  213.5 3.6 collective-permute-start
  215.7 226.0 %collective-permute-start.6 = (bf16[2,2,24,256]{3,2,1,0:T(8,128)(2,1)S(1)}, bf16[2,2,24,256]{3,2,1,0:T(8,128)(2,1)S(1)}, u32[]{:S(2)}, u32[]{:S(2)}) collective-permute-start(bf16[2,2,24,256]{3,2,1,0:T(8,128)(2,1)S(1)} %slice.810), channel_id=1, source_target_pairs={{4,0},{8,4},{12,8},{16,12},{20,16},{24,20},{28,24},{32,28},{36,32}... | collective-permute-start | bytes 147464 | tf_op jit(solution)/shard_map/ppermute | solution.py:23
  217.1 218.0 %collective-permute-start.2 = (bf16[1,2,26,384]{3,2,1,0:T(8,128)(2,1)S(1)}, bf16[1,2,26,384]{3,2,1,0:T(8,128)(2,1)S(1)}, u32[]{:S(2)}, u32[]{:S(2)}) collective-permute-start(bf16[1,2,26,384]{3,2,1,0:T(8,128)(2,1)S(1)} %pad_maximum_fusion.7), channel_id=1, source_target_pairs={{0,4},{4,8},{8,12},{12,16},{16,20},{20,24},{24,28},{28,32},{32,36}... | collective-permute-start | bytes 119816 | tf_op jit(solution)/shard_map/ppermute | solution.py:23
  441.7 11.2 %collective-permute-start.8 = (bf16[8,2,1,256]{3,2,1,0:T(2,128)(2,1)S(1)}, bf16[8,2,1,256]{3,2,1,0:T(2,128)(2,1)S(1)}, u32[]{:S(2)}, u32[]{:S(2)}) collective-permute-start(bf16[8,2,1,256]{3,2,1,0:T(2,128)(2,1)S(1)} %get-tuple-element.141), channel_id=1, source_target_pairs={{1,0},{2,1},{3,2},{5,4},{6,5},{7,6},{9,8},{10,9},{11,10},{13,12},{... | collective-permute-start | bytes 24584 | tf_op jit(solution)/shard_map/ppermute | solution.py:15
  449.6 3.4 collective-permute-start.7
  835.7 13.6 %copy-start.14 = (bf16[3,2,24,384]{3,2,1,0:T(8,128)(2,1)S(1)}, bf16[3,2,24,384]{3,2,1,0:T(8,128)(2,1)}, u32[]{:S(2)}) copy-start(bf16[3,2,24,384]{3,2,1,0:T(8,128)(2,1)} %get-tuple-element.154) | copy-start | bytes 331780
  835.7 13.6 %copy-start.29 = (bf16[1,1,1,384,256]{4,3,2,1,0:T(8,128)(2,1)S(1)}, bf16[1,1,1,384,256]{4,3,2,1,0:T(8,128)(2,1)}, u32[]{:S(2)}) copy-start(bf16[1,1,1,384,256]{4,3,2,1,0:T(8,128)(2,1)} %copy.83) | copy-start | bytes 589828
  835.7 13.8 %copy-start.23 = (bf16[1,1,1,384,256]{4,3,2,1,0:T(8,128)(2,1)S(1)}, bf16[1,1,1,384,256]{4,3,2,1,0:T(8,128)(2,1)}, u32[]{:S(2)}) copy-start(bf16[1,1,1,384,256]{4,3,2,1,0:T(8,128)(2,1)} %copy.92) | copy-start | bytes 589828
  835.7 14.0 %copy-start.22 = (bf16[1,1,1,384,256]{4,3,2,1,0:T(8,128)(2,1)S(1)}, bf16[1,1,1,384,256]{4,3,2,1,0:T(8,128)(2,1)}, u32[]{:S(2)}) copy-start(bf16[1,1,1,384,256]{4,3,2,1,0:T(8,128)(2,1)} %copy.94) | copy-start | bytes 589828
  853.6 36.5 %copy-start.13 = (bf16[1,1,1,256,256]{3,2,1,0,4:T(2,128)(2,1)S(1)}, bf16[1,1,1,256,256]{3,2,1,0,4:T(2,128)(2,1)}, u32[]{:S(2)}) copy-start(bf16[1,1,1,256,256]{3,2,1,0,4:T(2,128)(2,1)} %get-tuple-element.35) | copy-start | bytes 393220
  853.6 37.3 %copy-start.12 = (bf16[1,1,1,256,256]{3,2,1,0,4:T(2,128)(2,1)S(1)}, bf16[1,1,1,256,256]{3,2,1,0,4:T(2,128)(2,1)}, u32[]{:S(2)}) copy-start(bf16[1,1,1,256,256]{3,2,1,0,4:T(2,128)(2,1)} %get-tuple-element.34) | copy-start | bytes 393220
  853.6 38.2 %collective-permute-start.9 = (bf16[1,2,24,256]{3,2,1,0:T(8,128)(2,1)}, bf16[1,2,24,256]{3,2,1,0:T(8,128)(2,1)S(1)}, u32[]{:S(2)}, u32[]{:S(2)}) collective-permute-start(bf16[1,2,24,256]{3,2,1,0:T(8,128)(2,1)} %bitcast.167), channel_id=1, source_target_pairs={{4,0},{8,4},{12,8},{16,12},{20,16},{24,20},{28,24},{32,28},{36,32}... | collective-permute-start | bytes 73736 | tf_op jit(solution)/shard_map/ppermute | solution.py:23
  859.6 31.5 %copy-start.11 = (bf16[1,1,1,256,256]{3,2,1,0,4:T(2,128)(2,1)S(1)}, bf16[1,1,1,256,256]{3,2,1,0,4:T(2,128)(2,1)}, u32[]{:S(2)}) copy-start(bf16[1,1,1,256,256]{3,2,1,0,4:T(2,128)(2,1)} %get-tuple-element.33) | copy-start | bytes 393220
  859.6 31.6 %copy-start.10 = (bf16[1,1,1,256,256]{3,2,1,0,4:T(2,128)(2,1)S(1)}, bf16[1,1,1,256,256]{3,2,1,0,4:T(2,128)(2,1)}, u32[]{:S(2)}) copy-start(bf16[1,1,1,256,256]{3,2,1,0,4:T(2,128)(2,1)} %get-tuple-element.32) | copy-start | bytes 393220
  859.6 31.8 %copy-start.9 = (bf16[1,1,1,256,256]{3,2,1,0,4:T(2,128)(2,1)S(1)}, bf16[1,1,1,256,256]{3,2,1,0,4:T(2,128)(2,1)}, u32[]{:S(2)}) copy-start(bf16[1,1,1,256,256]{3,2,1,0,4:T(2,128)(2,1)} %get-tuple-element.31) | copy-start | bytes 393220
  859.6 31.9 %copy-start.8 = (bf16[1,1,1,256,256]{3,2,1,0,4:T(2,128)(2,1)S(1)}, bf16[1,1,1,256,256]{3,2,1,0,4:T(2,128)(2,1)}, u32[]{:S(2)}) copy-start(bf16[1,1,1,256,256]{3,2,1,0,4:T(2,128)(2,1)} %get-tuple-element.30) | copy-start | bytes 393220
  859.6 32.0 %copy-start.7 = (bf16[1,1,1,256,256]{3,2,1,0,4:T(2,128)(2,1)S(1)}, bf16[1,1,1,256,256]{3,2,1,0,4:T(2,128)(2,1)}, u32[]{:S(2)}) copy-start(bf16[1,1,1,256,256]{3,2,1,0,4:T(2,128)(2,1)} %get-tuple-element.29) | copy-start | bytes 393220
  859.6 32.2 %copy-start.5 = (bf16[288,256]{1,0:T(8,128)(2,1)S(1)}, bf16[288,256]{1,0:T(8,128)(2,1)}, u32[]{:S(2)}) copy-start(bf16[288,256]{1,0:T(8,128)(2,1)} %copy-done.4) | copy-start | bytes 442372
  861.5 44.1 %copy-start.3 = (f32[3,2,48,256]{3,2,1,0:T(8,128)S(1)}, f32[3,2,48,256]{3,2,1,0:T(8,128)}, u32[]{:S(2)}) copy-start(f32[3,2,48,256]{3,2,1,0:T(8,128)} %copy-done.2) | copy-start | bytes 884740
  871.6 42.7 %slice-start = ((s8[5308416]{0:T(1024)(128)(4,1)}), s8[1114112]{0:T(1024)(128)(4,1)S(1)}, s32[]{:S(2)}) async-start(s8[5308416]{0:T(1024)(128)(4,1)} %bitcast.575), calls=%async_computation.4 | async-start | bytes 2228224
  891.9 18.6 %collective-permute-start.11 = (bf16[7,2,1,256]{3,2,1,0:T(2,128)(2,1)S(1)}, bf16[7,2,1,256]{3,2,1,0:T(2,128)(2,1)S(1)}, u32[]{:S(2)}, u32[]{:S(2)}) collective-permute-start(bf16[7,2,1,256]{3,2,1,0:T(2,128)(2,1)S(1)} %get-tuple-element.164), channel_id=1, source_target_pairs={{1,0},{2,1},{3,2},{5,4},{6,5},{7,6},{9,8},{10,9},{11,10},{13,12},{... | collective-permute-start | bytes 21512 | tf_op jit(solution)/shard_map/ppermute | solution.py:15
  903.4 7.0 collective-permute-start.10
  905.7 14.7 %collective-permute-start.3 = (bf16[2,2,24,256]{3,2,1,0:T(8,128)(2,1)S(1)}, bf16[2,2,24,256]{3,2,1,0:T(8,128)(2,1)S(1)}, u32[]{:S(2)}, u32[]{:S(2)}) collective-permute-start(bf16[2,2,24,256]{3,2,1,0:T(8,128)(2,1)S(1)} %slice.956), channel_id=1, source_target_pairs={{0,4},{4,8},{8,12},{12,16},{16,20},{20,24},{24,28},{28,32},{32,36}... | collective-permute-start | bytes 147464 | tf_op jit(solution)/shard_map/ppermute | solution.py:23
  920.5 4.8 collective-permute-start.4
  923.3 5.1 collective-permute-start.5
  (66 other events, 453.7 us)
Sparse Core Ops, SparseCore 0:
  213.9 268.2 all-gather.4
  486.7 222.5 all-gather.6
